TPU v7x, 32 devices: a whole 2x2x4 slice. The times are simulated.
32 devices in a mesh: tx: 2 (over x), rx: 4 (over z), freq: 4 (over y, core).
Axes of the slice: x: 2, y: 2, z: 4, core: 2. Of those that a mesh axis runs over, the one named last changes fastest.
Arguments:
- spectrum: float32 [2, 8, 2048, 2048], P(None, 'freq', 'tx', 'rx'), may hold values from -6 to 6
- measured: float32 [2, 8, 2048, 2048], P(None, 'freq', 'tx', 'rx'), may hold values from -12 to 12
- wavenumber: float32 [8], replicated, may hold values from 1.5 to 3
- send_weight: float32 [2048], P('tx'), may hold values from 0.25 to 2
- hear_weight: float32 [2048], P('rx'), may hold values from 0.25 to 2
- aperture: int32 [128, 128], P('tx', 'rx'), may hold values 0 or 1
Outputs:
- updated: float32 [2, 8, 2048, 2048], P(None, 'freq', 'tx', 'rx')
- residual: float32 [2, 8, 2048, 2048], P(None, 'freq', 'tx', 'rx')
Inputs may be any that keep to these rules, and one draw needn't show every extreme that they name: `aperture`: 1 marks a live tile of 16 x 16 antenna pairs, 0 a silent one.
All inputs are finite; a program needn't handle non-finite values. No bound on the sum of `aperture` on one device may be relied on, other than what follows from the above.
Results may differ from a plain program's by a relative error of at most 0.00016.
Values sent between devices are 32-bit elements; how exact they have to be, the bound alone decides.
A program may use at most 192 MiB of HBM per device.

v0:
```python
import math

import jax
import jax.numpy as jnp
from jax import lax
from jax.sharding import PartitionSpec as P

depth_step = 2.0
step_size = 0.125
root_floor = 0.25
highest = lax.Precision.HIGHEST


def wave_numbers(offset, length, total):
    indices = offset + jnp.arange(length, dtype=jnp.int32)
    signed = jnp.where(indices < total // 2, indices, indices - total)
    return 2.0 * jnp.pi / total * signed.astype(jnp.float32)


def vertical(wavenumber, waves_sent, waves_heard):
    squared = (wavenumber * wavenumber)[:, None, None]
    first_root = jnp.sqrt(
        jnp.maximum(squared - (waves_sent * waves_sent)[None, :, None], 0.0) + root_floor
    )
    second_root = jnp.sqrt(
        jnp.maximum(squared - (waves_heard * waves_heard)[None, None, :], 0.0) + root_floor
    )
    return first_root + second_root


def unit_table(total, sign):
    indices = jnp.arange(total, dtype=jnp.int32)
    product = indices[:, None] * indices[None, :] % total
    phases = sign * 2.0 * math.pi / total * product.astype(jnp.float32)
    return (jnp.cos(phases), jnp.sin(phases))


def twiddle_table(outer, inner, sign):
    total = outer * inner
    product = (
        jnp.arange(outer, dtype=jnp.int32)[:, None]
        * jnp.arange(inner, dtype=jnp.int32)[None, :]
        % total
    )
    phases = sign * 2.0 * math.pi / total * product.astype(jnp.float32)
    return (jnp.cos(phases), jnp.sin(phases))


def complex_product(left_real, left_imag, table_real, table_imag, form):

    def einsum_of(operand, table):
        return jnp.einsum(form, operand, table, precision=highest)

    return (
        einsum_of(left_real, table_real) - einsum_of(left_imag, table_imag),
        einsum_of(left_real, table_imag) + einsum_of(left_imag, table_real),
    )


def split_length(total):
    inner = math.gcd(total, 128)
    return (total // inner, inner)


def transform_last(real_part, imag_part, sign):
    total = real_part.shape[-1]
    outer, inner = split_length(total)
    leading = real_part.shape[:-1]
    real_part = real_part.reshape(leading + (outer, inner))
    imag_part = imag_part.reshape(leading + (outer, inner))
    first_real, first_imag = unit_table(outer, sign)
    mixed_real, mixed_imag = complex_product(
        real_part, imag_part, first_real, first_imag, "...ab,ca->...cb"
    )
    twist_real, twist_imag = twiddle_table(outer, inner, sign)
    mixed_real, mixed_imag = (
        mixed_real * twist_real - mixed_imag * twist_imag,
        mixed_real * twist_imag + mixed_imag * twist_real,
    )
    second_real, second_imag = unit_table(inner, sign)
    final_real, final_imag = complex_product(
        mixed_real, mixed_imag, second_real, second_imag, "...cb,db->...dc"
    )
    scale = 1.0 / math.sqrt(total)
    return (
        (final_real * scale).reshape(leading + (total,)),
        (final_imag * scale).reshape(leading + (total,)),
    )


def transform_rows(real_part, imag_part, sign):
    turned_real = jnp.swapaxes(real_part, -1, -2)
    turned_imag = jnp.swapaxes(imag_part, -1, -2)
    done_real, done_imag = transform_last(turned_real, turned_imag, sign)
    return (jnp.swapaxes(done_real, -1, -2), jnp.swapaxes(done_imag, -1, -2))


def natural_columns(values, senders, hearers):
    leading = values.shape[:-1]
    width = values.shape[-1] // (senders * hearers)
    values = values.reshape(leading + (senders, hearers, width))
    values = jnp.swapaxes(values, -3, -2)
    return values.reshape(leading + (senders * hearers * width,))


def plane_transform(real_part, imag_part, sign):
    senders = lax.axis_size("tx")
    hearers = lax.axis_size("rx")
    rows_real, rows_imag = transform_rows(
        lax.all_to_all(real_part, "tx", split_axis=2, concat_axis=1, tiled=True),
        lax.all_to_all(imag_part, "tx", split_axis=2, concat_axis=1, tiled=True),
        sign,
    )
    spread_real = lax.all_to_all(rows_real, ("tx", "rx"), split_axis=1, concat_axis=2, tiled=True)
    spread_imag = lax.all_to_all(rows_imag, ("tx", "rx"), split_axis=1, concat_axis=2, tiled=True)
    spread_real = natural_columns(spread_real, senders, hearers)
    spread_imag = natural_columns(spread_imag, senders, hearers)
    done_real, done_imag = transform_last(spread_real, spread_imag, sign)
    return (
        lax.all_to_all(done_real, "rx", split_axis=2, concat_axis=1, tiled=True),
        lax.all_to_all(done_imag, "rx", split_axis=2, concat_axis=1, tiled=True),
    )


def per_device(spectrum, measured, wavenumber, send_weight, hear_weight, aperture):
    depth_local = spectrum.shape[1]
    rows_sent = spectrum.shape[2]
    rows_heard = spectrum.shape[3]
    freq_total = wavenumber.shape[0]
    senders = lax.axis_size("tx")
    hearers = lax.axis_size("rx")
    waves_sent = wave_numbers(lax.axis_index("tx") * rows_sent, rows_sent, rows_sent * senders)
    waves_heard = wave_numbers(lax.axis_index("rx") * rows_heard, rows_heard, rows_heard * hearers)
    vertical_waves = vertical(wavenumber, waves_sent, waves_heard)
    first_depth = lax.axis_index("freq") * depth_local
    cosine_layers = []
    sine_layers = []
    pair_real = jnp.zeros((freq_total, rows_sent, rows_heard), jnp.float32)
    pair_imag = jnp.zeros((freq_total, rows_sent, rows_heard), jnp.float32)
    for depth_index in range(depth_local):
        height = (first_depth + depth_index + 1).astype(jnp.float32) * depth_step
        phases = vertical_waves * height
        cosine = jnp.cos(phases)
        sine_part = jnp.sin(phases)
        cosine_layers.append(cosine)
        sine_layers.append(sine_part)
        layer_real = spectrum[0, depth_index][None]
        layer_imag = spectrum[1, depth_index][None]
        pair_real = pair_real + (cosine * layer_real + sine_part * layer_imag)
        pair_imag = pair_imag + (cosine * layer_imag - sine_part * layer_real)
    pair_real, pair_imag = (
        lax.psum_scatter(pair_real, "freq", scatter_dimension=0, tiled=True),
        lax.psum_scatter(pair_imag, "freq", scatter_dimension=0, tiled=True),
    )
    field_real, field_imag = plane_transform(pair_real, pair_imag, 1.0)
    tiles_sent, tiles_heard = aperture.shape
    gate = aperture.astype(jnp.float32)
    weights = (
        send_weight.reshape(tiles_sent, -1)[:, :, None, None]
        * gate[:, None, :, None]
        * hear_weight.reshape(tiles_heard, -1)[None, None, :, :]
    ).reshape(rows_sent, rows_heard)
    resid_real = weights[None] * (measured[0] - field_real)
    resid_imag = weights[None] * (measured[1] - field_imag)
    back_real, back_imag = plane_transform(resid_real, resid_imag, -1.0)
    piece_real = lax.all_gather(back_real, "freq", axis=0, tiled=True)
    piece_imag = lax.all_gather(back_imag, "freq", axis=0, tiled=True)
    layers_real = []
    layers_imag = []
    for depth_index in range(depth_local):
        cosine = cosine_layers[depth_index]
        sine_part = sine_layers[depth_index]
        layers_real.append(jnp.sum(cosine * piece_real - sine_part * piece_imag, axis=0))
        layers_imag.append(jnp.sum(cosine * piece_imag + sine_part * piece_real, axis=0))
    grad_real = jnp.stack(layers_real)
    grad_imag = jnp.stack(layers_imag)
    updated = spectrum + step_size * jnp.stack([grad_real, grad_imag])
    return (updated, jnp.stack([resid_real, resid_imag]))


def solution(mesh):
    placed = (
        P(None, "freq", "tx", "rx"),
        P(None, "freq", "tx", "rx"),
        P(),
        P("tx"),
        P("rx"),
        P("tx", "rx"),
    )
    return jax.shard_map(
        per_device,
        mesh=mesh,
        in_specs=placed,
        out_specs=(P(None, "freq", "tx", "rx"), P(None, "freq", "tx", "rx")),
        check_vma=False,
    )
```

profile of v0, /device:TPU:0, one launch (start us, length us, event | category | flops | bytes accessed | tf_op | source)
XLA Modules:
  0.0 1897.4 jit_solution(1728735074316996284)
XLA Ops:
  12.7 127.0 %fusion.23 = (f32[8,1024,512]{2,1,0:T(8,128)}, f32[8,1024,512]{2,1,0:T(8,128)}) fusion(f32[1024,512]{1,0:T(8,128)S(1)} %get-tuple-element.29, f32[1024,512]{1,0:T(8,128)S(1)} %get-tuple-element.27, f32[]{:T(128)S(6)} %mul.956, f32[1024,512]{1,0:T(8,128)S(1)} %get-tuple-element.28, f32[1024,512]{1,0:T(8,128)S(1)} %get-tuple-element.26, f32[]{:T(128)S(6)} %mul.928, ...), kind=kLoop, calls=%fused_computation.25 | loop fusion | flops 71303168 | bytes 41992200 | tf_op jit(solution)/shard_map/add | solution.py:150
  140.5 127.2 %reduce-scatter.3.cloned.1.call-done = f32[2,1024,512]{2,1,0:T(8,128)} async-done(((f32[8,1024,512]{2,1,0:T(8,128)}), f32[2,1024,512]{2,1,0:T(8,128)}) %reduce-scatter.3.cloned.1.call-update) | async-done | bytes 4194320 | tf_op jit(solution)/shard_map/reduce_scatter | solution.py:152
  280.8 114.5 %reduce-scatter.5.cloned.1.call-done = f32[2,1024,512]{2,1,0:T(8,128)} async-done(((f32[8,1024,512]{2,1,0:T(8,128)}), f32[2,1024,512]{2,1,0:T(8,128)}) %reduce-scatter.5.cloned.1.call-update) | async-done | bytes 4194320 | tf_op jit(solution)/shard_map/reduce_scatter | solution.py:153
  438.6 17.8 all-to-all-done.1
  499.2 12.2 copy.277
  531.5 12.3 copy.283
  543.8 65.5 %all-to-all-done.2 = f32[2,2048,256]{2,0,1:T(2,128)} async-done(((f32[2,2048,256]{2,0,1:T(2,128)}), f32[2,2048,256]{2,0,1:T(2,128)}, u32[]{:S(2)}, u32[]{:S(2)}) %all-to-all-start.2) | async-done | bytes 4194336 | tf_op jit(solution)/shard_map/all_to_all | solution.py:114
  641.5 64.7 %all-to-all-done.3 = f32[2,2048,256]{2,0,1:T(2,128)} async-done(((f32[2,2048,256]{2,0,1:T(2,128)}), f32[2,2048,256]{2,0,1:T(2,128)}, u32[]{:S(2)}, u32[]{:S(2)}) %all-to-all-start.3) | async-done | bytes 4194336 | tf_op jit(solution)/shard_map/all_to_all | solution.py:115
  746.7 12.2 copy.297
  779.3 12.2 copy.289
  791.5 62.9 %all-to-all-done.6 = f32[2,256,2048]{1,0,2:T(2,128)} async-done(((f32[2,256,2048]{1,0,2:T(2,128)}), f32[2,256,2048]{1,0,2:T(2,128)}, u32[]{:S(2)}, u32[]{:S(2)}) %all-to-all-start.6) | async-done | bytes 4194336 | tf_op jit(solution)/shard_map/all_to_all | solution.py:121
  868.3 14.9 mul.944
  894.8 57.2 %all-to-all-done.4 = f32[2,256,2048]{1,0,2:T(2,128)} async-done(((f32[2,256,2048]{1,0,2:T(2,128)}), f32[2,256,2048]{1,0,2:T(2,128)}, u32[]{:S(2)}, u32[]{:S(2)}) %all-to-all-start.4) | async-done | bytes 4194336 | tf_op jit(solution)/shard_map/all_to_all | solution.py:120
  993.9 40.3 %all-to-all-done.7 = f32[2,1024,512]{1,0,2:T(2,128)} async-done(((f32[2,1024,512]{1,0,2:T(2,128)}), f32[2,1024,512]{1,0,2:T(2,128)}, u32[]{:S(2)}, u32[]{:S(2)}) %all-to-all-start.7) | async-done | bytes 4194336 | tf_op jit(solution)/shard_map/all_to_all | solution.py:111
  1064.9 21.5 %all-to-all-done.5 = f32[2,1024,512]{1,0,2:T(2,128)} async-done(((f32[2,1024,512]{1,0,2:T(2,128)}), f32[2,1024,512]{1,0,2:T(2,128)}, u32[]{:S(2)}, u32[]{:S(2)}) %all-to-all-start.5) | async-done | bytes 4194336 | tf_op jit(solution)/shard_map/all_to_all | solution.py:110
  1130.9 12.2 copy.305
  1162.8 12.3 copy.311
  1175.1 64.9 %all-to-all-done.8 = f32[2,2048,256]{2,0,1:T(2,128)} async-done(((f32[2,2048,256]{2,0,1:T(2,128)}), f32[2,2048,256]{2,0,1:T(2,128)}, u32[]{:S(2)}, u32[]{:S(2)}) %all-to-all-start.8) | async-done | bytes 4194336 | tf_op jit(solution)/shard_map/all_to_all | solution.py:114
  1272.4 63.8 %all-to-all-done.9 = f32[2,2048,256]{2,0,1:T(2,128)} async-done(((f32[2,2048,256]{2,0,1:T(2,128)}), f32[2,2048,256]{2,0,1:T(2,128)}, u32[]{:S(2)}, u32[]{:S(2)}) %all-to-all-start.9) | async-done | bytes 4194336 | tf_op jit(solution)/shard_map/all_to_all | solution.py:115
  1387.2 93.9 %all_to_all.210 = f32[2,256,2048]{1,0,2:T(2,128)S(1)} all-to-all(f32[2,256,2048]{1,0,2:T(2,128)S(1)} %copy.317), channel_id=1, replica_groups=mesh['tx'=2,'rx'=4,'freq'=4] {'rx'}, dimensions={2} | all-to-all | bytes 8388608 | tf_op jit(solution)/shard_map/all_to_all | solution.py:120
  1514.7 94.6 %all_to_all.211 = f32[2,256,2048]{1,0,2:T(2,128)S(1)} all-to-all(f32[2,256,2048]{1,0,2:T(2,128)S(1)} %copy.323), channel_id=1, replica_groups=mesh['tx'=2,'rx'=4,'freq'=4] {'rx'}, dimensions={2} | all-to-all | bytes 8388608 | tf_op jit(solution)/shard_map/all_to_all | solution.py:121
  1625.8 15.0 subtract_multiply_fusion.1
  1648.8 73.6 %all-gather.5.cloned.1.call-done = f32[8,1024,512]{2,1,0:T(8,128)} async-done(((f32[2,1024,512]{2,1,0:T(8,128)}), f32[8,1024,512]{2,1,0:T(8,128)}) %all-gather.5.cloned.1.call-update) | async-done | bytes 16777232 | tf_op jit(solution)/shard_map/all_gather | solution.py:167
  1722.5 138.4 %fusion.31 = (f32[1024,512]{1,0:T(8,128)}, f32[1024,512]{1,0:T(8,128)S(1)}, f32[1024,512]{1,0:T(8,128)}, f32[1024,512]{1,0:T(8,128)}) fusion(f32[8,1024,512]{2,1,0:T(8,128)} %all-gather.5.cloned.1.call-done, f32[8,1024,512]{2,1,0:T(8,128)} %all-gather.3.cloned.1.call-done, f32[]{:T(128)S(6)} %mul.928, f32[8,512]{1,0:T(8,128)S(1)} %copy-done.29, ...), kind=kLoop, calls=%fused_computation.33 | loop fusion | flops 77594624 | bytes 41992200 | tf_op jit(solution)/shard_map/reduce_sum | solution.py:173
  (194 shorter events, 551.6 us)
Async XLA Ops:
  7.2 260.5 %reduce-scatter.3.cloned.1.call-start = ((), (), s32[]{:S(2)}) async-start(), calls=%async_computation.14 | async-start | bytes 20971520 | tf_op jit(solution)/shard_map/reduce_scatter | solution.py:152
  139.7 255.6 %reduce-scatter.5.cloned.1.call-start = ((), (), s32[]{:S(2)}) async-start(), calls=%async_computation.15 | async-start | bytes 20971520 | tf_op jit(solution)/shard_map/reduce_scatter | solution.py:153
  274.9 127.9 %all-to-all-start = ((f32[2,1024,512]{1,0,2:T(2,128)}), f32[2,1024,512]{1,0,2:T(2,128)}, u32[]{:S(2)}, u32[]{:S(2)}) async-start(f32[2,1024,512]{1,0,2:T(2,128)} %copy.266), calls=%async_computation.1 | async-start | bytes 8388608 | tf_op jit(solution)/shard_map/all_to_all | solution.py:110
  402.8 53.6 %all-to-all-start.1 = ((f32[2,1024,512]{1,0,2:T(2,128)}), f32[2,1024,512]{1,0,2:T(2,128)}, u32[]{:S(2)}, u32[]{:S(2)}) async-start(f32[2,1024,512]{1,0,2:T(2,128)} %copy.270), calls=%async_computation.3 | async-start | bytes 8388608 | tf_op jit(solution)/shard_map/all_to_all | solution.py:111
  425.3 8.0 copy-start.13
  472.9 7.8 copy-start.12
  472.9 7.8 copy-start.23
  511.4 97.9 %all-to-all-start.2 = ((f32[2,2048,256]{2,0,1:T(2,128)}), f32[2,2048,256]{2,0,1:T(2,128)}, u32[]{:S(2)}, u32[]{:S(2)}) async-start(f32[2,2048,256]{2,0,1:T(2,128)} %copy.277), calls=%async_computation.4 | async-start | bytes 8388608 | tf_op jit(solution)/shard_map/all_to_all | solution.py:114
  609.3 96.9 %all-to-all-start.3 = ((f32[2,2048,256]{2,0,1:T(2,128)}), f32[2,2048,256]{2,0,1:T(2,128)}, u32[]{:S(2)}, u32[]{:S(2)}) async-start(f32[2,2048,256]{2,0,1:T(2,128)} %copy.283), calls=%async_computation.5 | async-start | bytes 8388608 | tf_op jit(solution)/shard_map/all_to_all | solution.py:115
  628.1 8.0 copy-start.14
  759.0 95.5 %all-to-all-start.6 = ((f32[2,256,2048]{1,0,2:T(2,128)}), f32[2,256,2048]{1,0,2:T(2,128)}, u32[]{:S(2)}, u32[]{:S(2)}) async-start(f32[2,256,2048]{1,0,2:T(2,128)} %copy.297), calls=%async_computation.8 | async-start | bytes 8388608 | tf_op jit(solution)/shard_map/all_to_all | solution.py:121
  791.5 67.8 %copy-start.30 = (s32[64,32]{0,1:T(8,128)S(1)}, s32[64,32]{0,1:T(8,128)}, u32[]{:S(2)}) copy-start(s32[64,32]{0,1:T(8,128)} %param.11) | copy-start | bytes 24580
  791.5 67.9 %copy-start.31 = (f32[1024]{0:T(1024)S(1)}, f32[1024]{0:T(1024)}, u32[]{:S(2)}) copy-start(f32[1024]{0:T(1024)} %param.9) | copy-start | bytes 12292
  854.4 97.7 %all-to-all-start.4 = ((f32[2,256,2048]{1,0,2:T(2,128)}), f32[2,256,2048]{1,0,2:T(2,128)}, u32[]{:S(2)}, u32[]{:S(2)}) async-start(f32[2,256,2048]{1,0,2:T(2,128)} %copy.289), calls=%async_computation.6 | async-start | bytes 8388608 | tf_op jit(solution)/shard_map/all_to_all | solution.py:120
  868.3 14.9 copy-start.32
  980.9 53.3 %all-to-all-start.7 = ((f32[2,1024,512]{1,0,2:T(2,128)}), f32[2,1024,512]{1,0,2:T(2,128)}, u32[]{:S(2)}, u32[]{:S(2)}) async-start(f32[2,1024,512]{1,0,2:T(2,128)} %copy.300), calls=%async_computation.9 | async-start | bytes 8388608 | tf_op jit(solution)/shard_map/all_to_all | solution.py:111
  1034.2 52.2 %all-to-all-start.5 = ((f32[2,1024,512]{1,0,2:T(2,128)}), f32[2,1024,512]{1,0,2:T(2,128)}, u32[]{:S(2)}, u32[]{:S(2)}) async-start(f32[2,1024,512]{1,0,2:T(2,128)} %copy.292), calls=%async_computation.7 | async-start | bytes 8388608 | tf_op jit(solution)/shard_map/all_to_all | solution.py:110
  1143.1 96.8 %all-to-all-start.8 = ((f32[2,2048,256]{2,0,1:T(2,128)}), f32[2,2048,256]{2,0,1:T(2,128)}, u32[]{:S(2)}, u32[]{:S(2)}) async-start(f32[2,2048,256]{2,0,1:T(2,128)} %copy.305), calls=%async_computation.10 | async-start | bytes 8388608 | tf_op jit(solution)/shard_map/all_to_all | solution.py:114
  1239.9 96.2 %all-to-all-start.9 = ((f32[2,2048,256]{2,0,1:T(2,128)}), f32[2,2048,256]{2,0,1:T(2,128)}, u32[]{:S(2)}, u32[]{:S(2)}) async-start(f32[2,2048,256]{2,0,1:T(2,128)} %copy.311), calls=%async_computation.11 | async-start | bytes 8388608 | tf_op jit(solution)/shard_map/all_to_all | solution.py:115
  1244.5 404.3 %all-gather.3.cloned.1.call-start = ((), (), s32[]{:S(2)}) async-start(), calls=%async_computation.16 | async-start | bytes 20971520 | tf_op jit(solution)/shard_map/all_gather | solution.py:166
  1259.1 8.0 copy-start.15
  1488.7 233.8 %all-gather.5.cloned.1.call-start = ((), (), s32[]{:S(2)}) async-start(), calls=%async_computation.17 | async-start | bytes 20971520 | tf_op jit(solution)/shard_map/all_gather | solution.py:167
  1640.8 81.7 %copy-start.27 = (f32[8,1024]{1,0:T(8,128)S(1)}, f32[8,1024]{1,0:T(8,128)}, u32[]{:S(2)}) copy-start(f32[8,1024]{1,0:T(8,128)} %copy-done.26) | copy-start | bytes 98308
  1640.8 81.7 %copy-start.29 = (f32[8,512]{1,0:T(8,128)S(1)}, f32[8,512]{1,0:T(8,128)}, u32[]{:S(2)}) copy-start(f32[8,512]{1,0:T(8,128)} %copy-done.28) | copy-start | bytes 49156
  (25 other events, 136.7 us)
Sparse Core Ops, SparseCore 0:
  139.8 127.7 reduce-scatter.2
  270.2 125.0 reduce-scatter.4
  1488.8 104.7 all-gather.2
  1617.1 105.3 all-gather.4
where the time goes:
time: 1910 us; the launch traced here: 1900 us
  waiting for transfers between devices  774 us (41%)
  local copies, waits for them, and re-layouts  366 us (19%)
  other arithmetic  311 us (16%)
  matrix products  191 us (10%)
  blocking collectives  189 us (10%)
  starting transfers between devices  52.5 us (3%)
    dot_general x32, matrix products, einsum_of(): return jnp.einsum(form, operand, table, precision=highest)  191 us
    reduce_sum x1, other arithmetic, per_device(): jnp.sum(cosine * piece_real - sine_part * piece_imag, axis=0)  138 us
    all_to_all x2, waiting for transfers between devices, plane_transform(): lax.all_to_all(rows_real, ('tx', 'rx'), split_axis=1, concat_axis=2, tile...  130 us
    all_to_all x2, waiting for transfers between devices, plane_transform(): lax.all_to_all(rows_imag, ('tx', 'rx'), split_axis=1, concat_axis=2, tile...  128 us
    reduce_scatter x1, waiting for transfers between devices, per_device(): lax.psum_scatter(pair_real, 'freq', scatter_dimension=0, tiled=True)  127 us
    add x1, other arithmetic, per_device(): pair_imag = pair_imag + (cosine * layer_imag - sine_part * layer_real)  127 us
    reduce_scatter x1, waiting for transfers between devices, per_device(): lax.psum_scatter(pair_imag, 'freq', scatter_dimension=0, tiled=True)  114 us
    all_to_all x1, blocking collectives, plane_transform(): lax.all_to_all(done_imag, 'rx', split_axis=2, concat_axis=1, tiled=True)  94.6 us
  transfers between devices with their start and end apart: 14, of which 12 were waited for; matrix products, arithmetic and copies ran while one was open for 16% of the time, Pallas kernels for 0%

commit v1 on v0

v1 whole, which is shorter than its diff:
```python
import math

import jax
import jax.numpy as jnp
from jax import lax
from jax.experimental import pallas as pl
from jax.sharding import PartitionSpec as P

depth_step = 2.0
step_size = 0.125
root_floor = 0.25
radix = 4


def roots(wavenumber, offset, length, total):
    indices = offset + jnp.arange(length, dtype=jnp.int32)
    signed = jnp.where(indices < total // 2, indices, indices - total)
    waves = 2.0 * jnp.pi / total * signed.astype(jnp.float32)
    squared = (wavenumber * wavenumber)[:, None] - (waves * waves)[None, :]
    return jnp.sqrt(jnp.maximum(squared, 0.0) + root_floor)


def unit_pair(outer, inner, period):
    product = (
        jnp.arange(outer, dtype=jnp.int32)[:, None] * jnp.arange(inner, dtype=jnp.int32)[None, :] % period
    )
    phases = 2.0 * math.pi / period * product.astype(jnp.float32)
    return jnp.cos(phases), jnp.sin(phases)


def dft_tables(total):
    width = total // radix
    base_cos, base_sin = unit_pair(width, width, width)
    turn_cos, turn_sin = unit_pair(radix, width, total)
    scale = 1.0 / math.sqrt(total)
    turn_cos = turn_cos[:, None, :] * scale
    turn_sin = turn_sin[:, None, :] * scale
    return (
        turn_cos * base_cos - turn_sin * base_sin,
        turn_cos * base_sin + turn_sin * base_cos,
    )


def dft(pieces, tables, form, sign):
    (ar, ai), (br, bi), (cr, ci), (dr, di) = [(x[0], x[1]) for x in pieces]
    er, ei, gr, gi = ar + cr, ai + ci, ar - cr, ai - ci
    hr, hi, kr, ki = br + dr, bi + di, sign * (br - dr), sign * (bi - di)
    mixed_real = jnp.stack([er + hr, gr - ki, er - hr, gr + ki])
    mixed_imag = jnp.stack([ei + hi, gi + kr, ei - hi, gi - kr])
    mixed = jnp.stack([mixed_real, mixed_imag], axis=1)
    cosine, sine = tables
    first = jnp.einsum(form, cosine, mixed, precision=lax.Precision.HIGH)
    second = jnp.einsum(form, sine, mixed, precision=lax.Precision.HIGH)
    return jnp.stack(
        [
            first[:, :, 0] - sign * second[:, :, 1],
            first[:, :, 1] + sign * second[:, :, 0],
        ]
    )


def unmix(done, blocks):
    total = done.shape[1] * done.shape[2]
    rows = total // math.prod(blocks)
    freqs, width = done.shape[3:]
    done = jnp.transpose(done, (2, 1, 0, 3, 4)).reshape((math.prod(blocks), rows, 2, freqs, width))
    return jnp.transpose(done, (0, 2, 3, 1, 4)).reshape(tuple(blocks) + (2, freqs, rows, width))


def quarters(chunks, axis):
    count = chunks.shape[0]
    if count >= radix and count % radix == 0:
        step = count // radix
        return [
            jnp.concatenate([chunks[q * step + k] for k in range(step)], axis=axis) for q in range(radix)
        ]
    whole = jnp.concatenate([chunks[k] for k in range(count)], axis=axis)
    return jnp.split(whole, radix, axis=axis)


def exchange(values, axes):
    return lax.all_to_all(values, axes, split_axis=0, concat_axis=0, tiled=True)


def pair_kernel(layers, sent, heard, out):
    depth, rows = layers.shape[1:3]
    for f in range(out.shape[1]):
        hr = heard[0, f : f + 1, :]
        hi = heard[1, f : f + 1, :]
        for start in range(0, rows, 8):
            block = slice(start, start + 8)
            sr = sent[0, block, f : f + 1]
            si = sent[1, block, f : f + 1]
            zr = sr * hr - si * hi
            zi = -(sr * hi + si * hr)
            ar = layers[0, depth - 1, block, :]
            ai = layers[1, depth - 1, block, :]
            for j in range(depth - 1, -1, -1):
                ar, ai = ar * zr - ai * zi, ar * zi + ai * zr
                if j:
                    ar = ar + layers[0, j - 1, block, :]
                    ai = ai + layers[1, j - 1, block, :]
            out[0, f, block, :] = ar
            out[1, f, block, :] = ai


def gradient_kernel(pieces, sent, heard, out):
    freqs, rows = pieces.shape[1:3]
    depth = out.shape[1]
    for start in range(0, rows, 8):
        block = slice(start, start + 8)
        sums = [None] * depth
        for f in range(freqs):
            hr = heard[0, f : f + 1, :]
            hi = heard[1, f : f + 1, :]
            sr = sent[0, block, f : f + 1]
            si = sent[1, block, f : f + 1]
            zr = sr * hr - si * hi
            zi = sr * hi + si * hr
            tr = step_size * pieces[0, f, block, :]
            ti = step_size * pieces[1, f, block, :]
            for j in range(depth):
                tr, ti = tr * zr - ti * zi, tr * zi + ti * zr
                if f:
                    sums[j] = (sums[j][0] + tr, sums[j][1] + ti)
                else:
                    sums[j] = (tr, ti)
        for j in range(depth):
            out[0, j, block, :] = sums[j][0]
            out[1, j, block, :] = sums[j][1]


def pointwise(kernel, values, sent, heard, planes):
    _, count, rows, width = values.shape
    freqs = heard.shape[1]
    height = min(rows, 32)
    lanes = min(width, 128)
    return pl.pallas_call(
        kernel,
        grid=(rows // height, width // lanes),
        in_specs=[
            pl.BlockSpec((2, count, height, lanes), lambda i, k: (0, 0, i, k)),
            pl.BlockSpec((2, height, freqs), lambda i, k: (0, i, 0)),
            pl.BlockSpec((2, freqs, lanes), lambda i, k: (0, 0, k)),
        ],
        out_specs=pl.BlockSpec((2, planes, height, lanes), lambda i, k: (0, 0, i, k)),
        out_shape=jax.ShapeDtypeStruct((2, planes, rows, width), jnp.float32),
    )(values, sent, heard)


def per_device(spectrum, measured, wavenumber, send_weight, hear_weight, aperture):
    _, depth_local, rows_sent, rows_heard = spectrum.shape
    freq_local = measured.shape[1]
    freq_total = wavenumber.shape[0]
    senders = lax.axis_size("tx")
    hearers = lax.axis_size("rx")
    layers = lax.axis_size("freq")
    depth = depth_local * layers
    total_sent = rows_sent * senders
    total_heard = rows_heard * hearers
    slab = rows_sent // layers
    strip = rows_heard // senders
    band = rows_sent // hearers

    first_row = lax.axis_index("tx") * rows_sent + lax.axis_index("freq") * slab
    sent_phase = depth_step * roots(wavenumber, first_row, slab, total_sent).T
    heard_phase = depth_step * roots(wavenumber, lax.axis_index("rx") * rows_heard, rows_heard, total_heard)
    sent = jnp.stack([jnp.cos(sent_phase), jnp.sin(sent_phase)])
    heard = jnp.stack([jnp.cos(heard_phase), jnp.sin(heard_phase)])
    tables_sent = dft_tables(total_sent)
    tables_heard = tables_sent if total_heard == total_sent else dft_tables(total_heard)
    near = "qsm,qcfmw->qscfw"
    far = "qsm,qcfwm->qscfw"

    split = spectrum.reshape(2, depth_local, layers, slab, rows_heard)
    split = exchange(jnp.transpose(split, (2, 0, 1, 3, 4)), "freq")
    stacked = jnp.transpose(split, (1, 0, 2, 3, 4)).reshape(2, depth, slab, rows_heard)
    pair = pointwise(pair_kernel, stacked, sent, heard, freq_total)

    pair = pair.reshape(2, layers, freq_local, slab, senders, strip)
    pair = jnp.transpose(pair, (4, 1, 0, 2, 3, 5)).reshape(senders * layers, 2, freq_local, slab, strip)
    pair = exchange(pair, ("tx", "freq"))
    done = dft(quarters(pair, 2), tables_sent, near, 1.0)
    done = exchange(unmix(done, (senders * hearers,)), ("tx", "rx"))
    done = done.reshape((senders, hearers) + done.shape[1:])
    done = jnp.swapaxes(done, 0, 1).reshape((senders * hearers,) + done.shape[2:])
    done = dft(quarters(done, 3), tables_heard, far, 1.0)
    done = exchange(unmix(done, (hearers,)), "rx")
    field = jnp.transpose(done, (1, 2, 0, 4, 3)).reshape(2, freq_local, rows_sent, rows_heard)

    tiles_sent, tiles_heard = aperture.shape
    gate = aperture.astype(jnp.float32)
    weights = (
        send_weight.reshape(tiles_sent, -1)[:, :, None, None]
        * gate[:, None, :, None]
        * hear_weight.reshape(tiles_heard, -1)[None, None, :, :]
    ).reshape(rows_sent, rows_heard)
    residual = weights[None, None] * (measured - field)

    back = residual.reshape(2, freq_local, hearers, band, rows_heard)
    back = exchange(jnp.transpose(back, (2, 0, 1, 3, 4)), "rx")
    done = dft(quarters(back, 3), tables_heard, far, -1.0)
    done = unmix(done, (hearers, senders))
    done = jnp.swapaxes(done, 0, 1).reshape((senders * hearers,) + done.shape[2:])
    done = exchange(done, ("tx", "rx"))
    done = dft(quarters(done, 3), tables_sent, far, -1.0)
    done = exchange(unmix(done, (senders * layers,)), ("tx", "freq"))
    done = done.reshape(senders, layers, 2, freq_local, slab, strip)
    pieces = jnp.transpose(done, (2, 1, 3, 4, 0, 5)).reshape(2, freq_total, slab, rows_heard)

    gradient = pointwise(gradient_kernel, pieces, sent, heard, depth)
    gradient = gradient.reshape(2, layers, depth_local, slab, rows_heard)
    gradient = exchange(jnp.transpose(gradient, (1, 0, 2, 3, 4)), "freq")
    gradient = jnp.transpose(gradient, (1, 2, 0, 3, 4)).reshape(spectrum.shape)
    return (spectrum + gradient, residual)


def solution(mesh):
    placed = (
        P(None, "freq", "tx", "rx"),
        P(None, "freq", "tx", "rx"),
        P(),
        P("tx"),
        P("rx"),
        P("tx", "rx"),
    )
    return jax.shard_map(
        per_device,
        mesh=mesh,
        in_specs=placed,
        out_specs=(P(None, "freq", "tx", "rx"), P(None, "freq", "tx", "rx")),
        check_vma=False,
    )
```

time: 1910 us -> 1460 us (0.76)
  blocking collectives: 189 us -> 754 us
  waiting for transfers between devices: 774 us -> 336 us
  other arithmetic: 311 us -> 73.6 us
  local copies, waits for them, and re-layouts: 366 us -> 156 us
  matrix products: 191 us -> 58.1 us
  Pallas kernels: 0 us -> 49.4 us
  starting transfers between devices: 52.5 us -> 16.8 us
    all_to_all x2 -> x5, blocking collectives: 189 us -> 754 us  [exchange(): return lax.all_to_all(values, axes, split_axis=0, concat_axis=0, tiled=True)]
    reduce_scatter x2 -> x0, waiting for transfers between devices: 242 us -> none  [the longest x1 127 us: per_device(): lax.psum_scatter(pair_real, 'freq', scatter_dimension=0, tiled=True)]
    reduce_sum x1 -> x0, other arithmetic: 138 us -> none  [per_device(): jnp.sum(cosine * piece_real - sine_part * piece_imag, axis=0)]
    dot_general x32 -> x8, matrix products: 191 us -> 58.1 us  [the longest x4 29.3 us: dft(): first = jnp.einsum(form, cosine, mixed, precision=lax.Precision.HIGH)]
    all_to_all x10 -> x3, waiting for transfers between devices: 458 us -> 336 us  [exchange(): return lax.all_to_all(values, axes, split_axis=0, concat_axis=0, tiled=True)]
    add x2 -> x11, other arithmetic: 131 us -> 21 us  [the longest x1 11.3 us: per_device(): return (spectrum + gradient, residual)]
    all_to_all x20 -> x3, local copies, waits for them, and re-layouts: 94.7 us -> 7.27 us  [exchange(): return lax.all_to_all(values, axes, split_axis=0, concat_axis=0, tiled=True)]
    all_gather x2 -> x0, waiting for transfers between devices: 73.6 us -> none  [the longest x1 73.6 us: per_device(): piece_imag = lax.all_gather(back_imag, 'freq', axis=0, tiled=True)]
  transfers between devices with their start and end apart: 14 -> 3, of which waited for: 12 -> 3; matrix products, arithmetic and copies ran while one was open for 16% -> 2% of each run, Pallas kernels for 0% -> 0%
where the time goes in v1:
time: 1460 us; the launch traced here: 1450 us
  blocking collectives  754 us (52%)
  waiting for transfers between devices  336 us (23%)
  local copies, waits for them, and re-layouts  156 us (11%)
  other arithmetic  73.6 us (5%)
  matrix products  58.1 us (4%)
  Pallas kernels  49.4 us (3%)
  starting transfers between devices  16.8 us (1%)
    all_to_all x5, blocking collectives, exchange(): return lax.all_to_all(values, axes, split_axis=0, concat_axis=0, tiled=True)  754 us
    all_to_all x3, waiting for transfers between devices, exchange(): return lax.all_to_all(values, axes, split_axis=0, concat_axis=0, tiled=True)  336 us
    pallas_call x2, Pallas kernels, pointwise(): pl.pallas_call(kernel, grid=(rows // height, width // lanes), in_specs=[p...  49.4 us
    transpose x4, local copies, waits for them, and re-layouts, unmix(): jnp.transpose(done, (2, 1, 0, 3, 4))  38.8 us
    dot_general x4, matrix products, dft(): first = jnp.einsum(form, cosine, mixed, precision=lax.Precision.HIGH)  29.3 us
  transfers between devices with their start and end apart: 3, of which 3 were waited for; matrix products, arithmetic and copies ran while one was open for 2% of the time, Pallas kernels for 0%

profile of v1, /device:TPU:0, one launch (start us, length us, event | category | flops | bytes accessed | tf_op | source)
XLA Modules:
  0.0 1445.1 jit_solution(16936419594886305284)
XLA Ops:
  0.6 8.1 copy.126
  16.4 92.0 %all-to-all-done = f32[4,2,2,256,512]{4,3,2,1,0:T(8,128)} async-done(((f32[4,2,2,256,512]{4,3,2,1,0:T(8,128)}), f32[4,2,2,256,512]{4,3,2,1,0:T(8,128)}, u32[]{:S(2)}, u32[]{:S(2)}) %all-to-all-start) | async-done | bytes 8388640 | tf_op jit(solution)/shard_map/all_to_all | solution.py:82
  108.4 8.1 copy.127
  116.5 24.7 %shard_map.77 = f32[2,8,256,512]{3,2,1,0:T(8,128)} custom-call(f32[2,8,256,512]{3,2,1,0:T(8,128)} %bitcast.225, f32[2,256,8]{2,1,0:T(8,128)} %copy.128.sent, f32[2,8,512]{2,1,0:T(8,128)} %pad_maximum_fusion.20.heard), custom_call_target="tpu_custom_call" | custom-call | tf_op jit(solution)/shard_map/pallas_call | solution.py:138
  141.2 10.5 reshape.804
  168.8 88.9 %all-to-all-done.1 = f32[8,2,2,256,256]{4,3,2,1,0:T(8,128)} async-done(((f32[8,2,2,256,256]{4,3,2,1,0:T(8,128)}), f32[8,2,2,256,256]{4,3,2,1,0:T(8,128)}, u32[]{:S(2)}, u32[]{:S(2)}) %all-to-all-start.1) | async-done | bytes 8388640 | tf_op jit(solution)/shard_map/all_to_all | solution.py:82
  288.6 9.2 copy.133
  297.9 189.6 %all_to_all.40 = f32[8,2,2,256,256]{4,2,1,3,0:T(2,128)S(1)} all-to-all(f32[8,2,2,256,256]{4,2,1,3,0:T(2,128)S(1)} %bitcast.227), channel_id=1, replica_groups=mesh['tx'=2,'rx'=4,'freq'=4] {'tx','rx'}, dimensions={0} | all-to-all | bytes 16777216 | tf_op jit(solution)/shard_map/all_to_all | solution.py:82
  514.6 11.1 copy.139
  532.1 8.5 mul.580
  540.6 14.9 %mul.581 = f32[1024,512]{1,0:T(8,128)} reshape(f32[64,16,32,16]{3,2,1,0:T(8,128)} %mul.580) | data formatting | bytes 4194304 | tf_op jit(solution)/shard_map/mul | solution.py:194
  558.7 154.9 %all-to-all-done.3 = f32[4,2,2,512,256]{4,2,1,3,0:T(2,128)} async-done(((f32[4,2,2,512,256]{4,2,1,3,0:T(2,128)}), f32[4,2,2,512,256]{4,2,1,3,0:T(2,128)}, u32[]{:S(2)}, u32[]{:S(2)}) %all-to-all-start.3) | async-done | bytes 8388640 | tf_op jit(solution)/shard_map/all_to_all | solution.py:82
  713.6 13.1 copy.140
  726.8 12.1 fusion
  743.3 185.3 %all_to_all.41 = f32[4,2,2,256,512]{4,3,2,1,0:T(8,128)S(1)} all-to-all(f32[4,2,2,256,512]{4,3,2,1,0:T(8,128)S(1)} %bitcast.235), channel_id=1, replica_groups=mesh['tx'=2,'rx'=4,'freq'=4] {'rx'}, dimensions={0} | all-to-all | bytes 16777216 | tf_op jit(solution)/shard_map/all_to_all | solution.py:82
  951.9 9.2 copy.147
  963.5 186.5 %all_to_all.42 = f32[8,2,2,256,256]{4,3,2,1,0:T(8,128)S(1)} all-to-all(f32[8,2,2,256,256]{4,3,2,1,0:T(8,128)S(1)} %bitcast.231), channel_id=1, replica_groups=mesh['tx'=2,'rx'=4,'freq'=4] {'tx','rx'}, dimensions={0} | all-to-all | bytes 16777216 | tf_op jit(solution)/shard_map/all_to_all | solution.py:82
  1177.0 9.2 copy.155
  1186.2 97.2 %all_to_all.43 = f32[8,2,2,256,256]{4,2,1,3,0:T(2,128)S(1)} all-to-all(f32[8,2,2,256,256]{4,2,1,3,0:T(2,128)S(1)} %bitcast.232), channel_id=1, replica_groups=mesh['tx'=2,'rx'=4,'freq'=4] {'tx','freq'}, dimensions={0} | all-to-all | bytes 16777216 | tf_op jit(solution)/shard_map/all_to_all | solution.py:82
  1284.9 8.0 copy.157
  1292.8 11.6 reshape.817.pieces
  1304.4 24.7 %shard_map.78 = f32[2,8,256,512]{3,2,1,0:T(8,128)} custom-call(f32[2,8,256,512]{3,2,1,0:T(8,128)} %reshape.817.pieces, f32[2,256,8]{2,1,0:T(8,128)} %copy.128.sent, f32[2,8,512]{2,1,0:T(8,128)} %pad_maximum_fusion.20.heard), custom_call_target="tpu_custom_call" | custom-call | tf_op jit(solution)/shard_map/pallas_call | solution.py:138
  1333.5 95.8 %all_to_all.44 = f32[4,2,2,256,512]{4,3,2,1,0:T(8,128)S(1)} all-to-all(f32[4,2,2,256,512]{4,3,2,1,0:T(8,128)S(1)} %bitcast.234), channel_id=1, replica_groups=mesh['tx'=2,'rx'=4,'freq'=4] {'freq'}, dimensions={0} | all-to-all | bytes 16777216 | tf_op jit(solution)/shard_map/all_to_all | solution.py:82
  1433.6 11.3 bitcast_add_fusion
  (78 shorter events, 159.0 us)
Async XLA Ops:
  8.8 5.8 copy-start.3
  8.8 99.7 %all-to-all-start = ((f32[4,2,2,256,512]{4,3,2,1,0:T(8,128)}), f32[4,2,2,256,512]{4,3,2,1,0:T(8,128)}, u32[]{:S(2)}, u32[]{:S(2)}) async-start(f32[4,2,2,256,512]{4,3,2,1,0:T(8,128)} %copy.126), calls=%async_computation | async-start | bytes 16777216 | tf_op jit(solution)/shard_map/all_to_all | solution.py:82
  159.7 98.1 %all-to-all-start.1 = ((f32[8,2,2,256,256]{4,3,2,1,0:T(8,128)}), f32[8,2,2,256,256]{4,3,2,1,0:T(8,128)}, u32[]{:S(2)}, u32[]{:S(2)}) async-start(f32[8,2,2,256,256]{4,3,2,1,0:T(8,128)} %bitcast.222), calls=%async_computation.1 | async-start | bytes 16777216 | tf_op jit(solution)/shard_map/all_to_all | solution.py:82
  525.7 6.0 copy-start
  525.7 6.1 copy-start.1
  525.7 188.0 %all-to-all-start.3 = ((f32[4,2,2,512,256]{4,2,1,3,0:T(2,128)}), f32[4,2,2,512,256]{4,2,1,3,0:T(2,128)}, u32[]{:S(2)}, u32[]{:S(2)}) async-start(f32[4,2,2,512,256]{4,2,1,3,0:T(2,128)} %bitcast.221), calls=%async_computation.3 | async-start | bytes 16777216 | tf_op jit(solution)/shard_map/all_to_all | solution.py:82
  540.6 14.9 %copy-start.2 = (f32[512]{0:T(512)S(1)}, f32[512]{0:T(512)}, u32[]{:S(2)}) copy-start(f32[512]{0:T(512)} %param.10) | copy-start | bytes 6148
